TPU v7x, 32 devices: a whole 2x2x4 slice. The times are simulated.
32 devices in a mesh: dp: 4 (over z), vocab: 8 (over y, x, core).
Axes of the slice: x: 2, y: 2, z: 4, core: 2. Of those that a mesh axis runs over, the one named last changes fastest.
Arguments:
- hidden: bfloat16 [2048, 5120], P('dp', 'vocab')
- weight: bfloat16 [5120, 19456], P(None, 'vocab'), may hold values from -0.078125 to 0.078125
- targets: int32 [2048], P('dp'), may hold values from 0 to 19455
- old_logprob: float32 [2048], P('dp'), may hold values from -13 to -10.5
- ref_logprob: float32 [2048], P('dp'), may hold values from -13 to -10.5
- lengths: int32 [32], P('dp'), may hold values from 1 to 64
- rewards: int32 [32], P('dp'), may hold values from 0 to 4
- group_ids: int32 [32], P('dp'), may hold values from 0 to 3, as said below
Outputs:
- token_logprob: float32 [2048], P('dp')
- entropy: float32 [2048], P('dp')
- advantage: float32 [2048], P('dp')
- loss: float32 [], replicated
Inputs may be any that keep to these rules, and one draw needn't show every extreme that they name: `group_ids`: each prompt number is named by exactly 8 rollouts.
All inputs are finite; a program needn't handle non-finite values.
Results may differ from a plain program's by a relative error of at most 0.0003.
Values may be sent and summed in bfloat16 or wider, within the bound.
A program may use at most 128 MiB of HBM per device.

v0:
```python
import jax
import jax.numpy as jnp
from jax import lax
from jax.sharding import PartitionSpec as P

GROUP = 8


def per_device(hidden, weight, targets, old_logprob, ref_logprob, lengths, rewards, group_ids):
    width = weight.shape[1]
    tok_rows = hidden.shape[0]
    offset = lax.axis_index("vocab") * width
    features_all = lax.all_gather(hidden, "vocab", axis=1, tiled=True)
    logits = jnp.dot(features_all, weight, preferred_element_type=jnp.float32)
    columns = lax.broadcasted_iota(jnp.int32, (1, width), 1) + offset
    picked = jnp.sum(jnp.where(columns == targets[:, None], logits, 0.0), axis=1)
    local_top = jnp.max(logits, axis=1)
    top = lax.pmax(local_top, "vocab")
    scaled = jnp.exp(logits - top[:, None])
    total, moment, target_logit = lax.psum(
        (jnp.sum(scaled, axis=1), jnp.sum(scaled * logits, axis=1), picked), "vocab"
    )
    lse = top + jnp.log(total)
    token_logprob = target_logit - lse
    entropy = lse - moment / total
    roll_rows = rewards.shape[0]
    prompt_count = roll_rows * lax.axis_size("dp") // GROUP
    member = (group_ids[:, None] == jnp.arange(prompt_count, dtype=jnp.int32)[None, :]).astype(
        jnp.float32
    )
    scores = rewards.astype(jnp.float32)
    part_sums = jnp.dot(scores, member, precision=lax.Precision.HIGHEST)
    part_squares = jnp.dot(scores * scores, member, precision=lax.Precision.HIGHEST)
    seq_len = tok_rows // roll_rows
    position = jnp.arange(seq_len, dtype=jnp.int32)
    mask = (position[None, :] < lengths[:, None]).astype(jnp.float32).reshape(tok_rows)
    local_count = jnp.sum(mask)
    sums, squares = lax.psum((part_sums, part_squares), "dp")
    mean = sums / GROUP
    spread = jnp.sqrt(jnp.maximum(squares / GROUP - mean * mean, 0.0))
    mean_roll = jnp.dot(member, mean, precision=lax.Precision.HIGHEST)
    spread_roll = jnp.dot(member, spread, precision=lax.Precision.HIGHEST)
    advantage = jnp.repeat((scores - mean_roll) / jnp.maximum(spread_roll, 1.0), seq_len)
    ratio = jnp.exp(jnp.clip(token_logprob - old_logprob, -20.0, 20.0))
    surrogate = -jnp.minimum(ratio * advantage, jnp.clip(ratio, 0.8, 1.2) * advantage)
    shift = jnp.clip(ref_logprob - token_logprob, -20.0, 20.0)
    divergence = jnp.exp(shift) - shift - 1.0
    local_numer = jnp.sum(mask * (surrogate + 0.04 * divergence - 0.01 * entropy))
    numer, count = lax.psum((local_numer, local_count), "dp")
    loss = numer / count
    return (token_logprob, entropy, advantage, loss)


def solution(mesh):
    return jax.shard_map(
        per_device,
        mesh=mesh,
        in_specs=(
            P("dp", "vocab"),
            P(None, "vocab"),
            P("dp"),
            P("dp"),
            P("dp"),
            P("dp"),
            P("dp"),
            P("dp"),
        ),
        out_specs=(P("dp"), P("dp"), P("dp"), P()),
        check_vma=False,
    )
```

profile of v0, /device:TPU:0, one launch (start us, length us, event | category | flops | bytes accessed | tf_op | source)
XLA Modules:
  0.0 127.2 jit_solution(17429354266710759954)
XLA Ops:
  7.2 0.0 all-gather.2.cloned.1.call-start
  7.2 0.7 all-gather.2.cloned.1.call-update
  7.9 0.9 convolution_bitcast_fusion.1
  8.8 0.9 convolution_bitcast_fusion.3
  9.6 13.5 %all-reduce.2 = (f32[4]{0:T(128)S(1)}, f32[4]{0:T(128)S(1)}) all-reduce(f32[4]{0:T(128)S(1)} %convolution_bitcast_fusion.1, f32[4]{0:T(128)S(1)} %convolution_bitcast_fusion.3), channel_id=1, replica_groups=mesh['dp'=4,'vocab'=8] {'dp'}, use_global_device_ids=true, to_apply=%region_9.10 | all-reduce | flops 8 | bytes 64 | tf_op jit(solution)/shard_map/psum | solution.py:38
  23.1 0.8 fusion.3
  23.9 0.9 fusion.2
  24.8 0.1 broadcast_in_dim.7
  24.9 0.1 reshape.24
  24.9 0.0 copy-start
  24.9 0.7 iota_compare_fusion
  25.7 0.1 lt.21
  25.8 1.4 %convert_reduce_fusion = f32[]{:T(128)} fusion(s32[8]{0:T(128)} %param.13), kind=kLoop, calls=%fused_computation.12 | loop fusion | flops 1535 | bytes 36 | tf_op jit(solution)/shard_map/reduce_sum | solution.py:37
  27.2 0.0 copy-start.1
  27.2 26.4 %all-gather.2.cloned.1.call-done = bf16[512,5120]{1,0:T(8,128)(2,1)} async-done(((bf16[512,640]{1,0:T(8,128)(2,1)}), bf16[512,5120]{1,0:T(8,128)(2,1)}) %all-gather.2.cloned.1.call-update) | async-done | bytes 5242896 | tf_op jit(solution)/shard_map/all_gather | solution.py:13
  53.5 21.8 %fusion.30 = (f32[512]{0:T(512)S(1)}, f32[512,2432]{1,0:T(8,128)}) fusion(bf16[512,5120]{1,0:T(8,128)(2,1)} %all-gather.2.cloned.1.call-done, bf16[5120,2432]{1,0:T(8,128)(2,1)} %param.9), kind=kOutput, calls=%fused_computation.46 | convolution fusion | flops 12751929344 | bytes 35129344 | tf_op jit(solution)/shard_map/dot_general | solution.py:14
  75.4 0.0 copy-start.2
  75.4 0.0 copy-start.3
  75.4 13.2 %pmax.7 = f32[512]{0:T(512)S(1)} all-reduce(f32[512]{0:T(512)S(1)} %get-tuple-element.17), channel_id=1, replica_groups=mesh['dp'=4,'vocab'=8] {'vocab'}, use_global_device_ids=true, to_apply=%region_3.4 | all-reduce | flops 512 | bytes 4096 | tf_op jit(solution)/shard_map/pmax | solution.py:18
  88.6 0.0 copy-done.1
  88.6 3.7 %multiply_reduce_fusion = (f32[512]{0:T(512)S(1)}, f32[512]{0:T(512)S(1)}, f32[512]{0:T(512)S(1)}) fusion(f32[512,2432]{1,0:T(8,128)} %get-tuple-element.18, f32[512]{0:T(512)S(1)} %pmax.7, s32[512]{0:T(512)S(1)} %copy-done.1, s32[2432]{0:T(1024)S(1)} %iota_add_fusion), kind=kLoop, calls=%fused_computation | loop fusion | flops 8714752 | bytes 5000704 | tf_op jit(solution)/shard_map/reduce_sum | solution.py:21
  92.3 12.0 %all-reduce = (f32[512]{0:T(512)S(1)}, f32[512]{0:T(512)S(1)}, f32[512]{0:T(512)S(1)}) all-reduce(f32[512]{0:T(512)S(1)} %get-tuple-element.6, f32[512]{0:T(512)S(1)} %get-tuple-element.5, f32[512]{0:T(512)S(1)} %get-tuple-element.4), channel_id=1, replica_groups=mesh['dp'=4,'vocab'=8] {'vocab'}, use_global_device_ids=true, to_apply=%region_1.2 | all-reduce | flops 1536 | bytes 12288 | tf_op jit(solution)/shard_map/psum | solution.py:20
  104.3 0.0 copy-done
  104.3 0.0 copy-done.2
  104.4 0.0 copy-done.3
  104.4 1.2 fusion.13
  105.6 12.4 %all-reduce.1 = (f32[]{:T(128)}, f32[]{:T(128)}) all-reduce(f32[]{:T(128)} %get-tuple-element.14, f32[]{:T(128)} %convert_reduce_fusion), channel_id=1, replica_groups=mesh['dp'=4,'vocab'=8] {'dp'}, use_global_device_ids=true, to_apply=%region_11.12 | all-reduce | flops 2 | bytes 16 | tf_op jit(solution)/shard_map/psum | solution.py:49
  (1 shorter events, 0.0 us)
Async XLA Ops:
  7.2 46.4 %all-gather.2.cloned.1.call-start = ((), (), s32[]{:S(2)}) async-start(), calls=%async_computation | async-start | bytes 5898240 | tf_op jit(solution)/shard_map/all_gather | solution.py:13
  24.9 79.4 %copy-start = (f32[512]{0:T(512)}, f32[512]{0:T(512)S(1)}, u32[]{:S(2)}) copy-start(f32[512]{0:T(512)S(1)} %reshape.24) | copy-start | bytes 6148
  27.2 61.4 %copy-start.1 = (s32[512]{0:T(512)S(1)}, s32[512]{0:T(512)}, u32[]{:S(2)}) copy-start(s32[512]{0:T(512)} %param.10) | copy-start | bytes 6148
  75.4 29.0 %copy-start.2 = (f32[512]{0:T(512)S(1)}, f32[512]{0:T(512)}, u32[]{:S(2)}) copy-start(f32[512]{0:T(512)} %param.12) | copy-start | bytes 6148
  75.4 29.0 %copy-start.3 = (f32[512]{0:T(512)S(1)}, f32[512]{0:T(512)}, u32[]{:S(2)}) copy-start(f32[512]{0:T(512)} %param.11) | copy-start | bytes 6148
Sparse Core Ops, SparseCore 0:
  9.9 43.6 all-gather.1
where the time goes:
time: 128 us; the launch traced here: 127 us
  blocking collectives  51.1 us (40%)
  waiting for transfers between devices  27.1 us (21%)
  matrix products  25.3 us (20%)
  between operations  16.5 us (13%)
  other arithmetic  7.03 us (5%)
    all_gather x1, waiting for transfers between devices, per_device(): features_all = lax.all_gather(hidden, 'vocab', axis=1, tiled=True)  26.4 us
    dot_general x1, matrix products, per_device(): logits = jnp.dot(features_all, weight, preferred_element_type=jnp.float32)  21.8 us
    psum x1, blocking collectives, per_device(): sums, squares = lax.psum((part_sums, part_squares), 'dp')  13.5 us
    pmax x1, blocking collectives, per_device(): top = lax.pmax(local_top, 'vocab')  13.2 us
    psum x1, blocking collectives, per_device(): numer, count = lax.psum((local_numer, local_count), 'dp')  12.4 us
    psum x1, blocking collectives, per_device(): lax.psum((jnp.sum(scaled, axis=1), jnp.sum(scaled * logits, axis=1), pick...  12 us
    reduce_sum x1, other arithmetic, per_device(): jnp.sum(scaled * logits, axis=1)  3.7 us
  transfers between devices with their start and end apart: 1, of which 1 were waited for; matrix products, arithmetic and copies ran while one was open for 5% of the time, Pallas kernels for 0%

commit v1 on v0

v1 whole, which is shorter than its diff:
```python
import functools

import jax
import jax.numpy as jnp
from jax import lax
from jax.experimental import pallas as pl
from jax.experimental.pallas import tpu as pltpu
from jax.sharding import PartitionSpec as P

GROUP = 8
LANES = 128
CHUNKS = 4
TILE = 512
MESH = pl.DeviceIdType.MESH


def kernel(n, dpn, h, w, tg, olp, rlp, lens, rew, gid, tok, ent, adv, loss,
           feats, wv, acc, tcol, part, st, dpa, dpb,
           hsem, wsem, ssem, rsem, st_s, st_r, dpa_s, dpa_r, dpb_s, dpb_r):
    me = lax.axis_index("vocab")
    my = lax.axis_index("dp")
    tokens, kdim = h.shape
    width = w.shape[1]
    nq = tokens // LANES
    nr = lens.shape[0]
    seq = tokens // nr
    grid = n == 8
    rows = tokens // CHUNKS

    if grid:
        core, cx, cy = me % 2, (me // 2) % 2, me // 4
        flip = 1 - 2 * core
        xn = (cy * 2 + (1 - cx)) * 2 + core
        yn = ((1 - cy) * 2 + cx) * 2 + core
        dn = ((1 - cy) * 2 + (1 - cx)) * 2 + core
        sib = me + flip
        owners = [me, sib, xn, xn + flip, yn, yn + flip, dn, dn + flip]

    def wcopy(slot, owner):
        return pltpu.make_async_copy(
            w.at[pl.ds(pl.multiple_of(owner * kdim, kdim), kdim), :], wv.at[slot], wsem.at[slot])

    def remote(src, dst, s, r, dev):
        return pltpu.make_async_remote_copy(
            src_ref=src, dst_ref=dst, send_sem=s, recv_sem=r,
            device_id=(my, dev), device_id_type=MESH)

    def todp(buf, s, r, dev):
        return pltpu.make_async_remote_copy(
            src_ref=buf.at[my], dst_ref=buf.at[my], send_sem=s.at[dev], recv_sem=r.at[my],
            device_id=(dev, me), device_id_type=MESH)

    hcopy = pltpu.make_async_copy(h, feats.at[0], hsem)
    hcopy.start()
    if grid:
        for s in range(n):
            wcopy(s, owners[s]).start()
    else:
        def wstart(s, c):
            wcopy(s, lax.rem(me - s + n, n)).start()
            return c
        lax.fori_loop(0, n, wstart, 0)

    barrier = pltpu.get_barrier_semaphore()
    for s in range(1, n):
        pl.semaphore_signal(barrier, inc=1, device_id=(my, lax.rem(me + s, n)), device_id_type=MESH)
    for s in range(1, dpn):
        pl.semaphore_signal(barrier, inc=1, device_id=(lax.rem(my + s, dpn), me), device_id_type=MESH)
    pl.semaphore_wait(barrier, n - 1 + dpn - 1)

    def span(r):
        return pl.ds(pl.multiple_of(r * rows, rows), rows)

    def half(r, i):
        return pl.ds(pl.multiple_of(r * rows + i * (rows // 2), rows // 2), rows // 2)

    def to_x(r):
        return remote(h.at[span(r)], feats.at[2, span(r)], ssem.at[2, r, 0], rsem.at[2, r, 0], xn)

    def to_y(r):
        return remote(h.at[span(r)], feats.at[4, span(r)], ssem.at[4, r, 0], rsem.at[4, r, 0], yn)

    def to_sib(slot, r):
        return remote(feats.at[slot, span(r)], feats.at[slot + 1, span(r)],
                      ssem.at[slot + 1, r, 0], rsem.at[slot + 1, r, 0], sib)

    def own_sib():
        return remote(h, feats.at[1], ssem.at[1, 0, 0], rsem.at[1, 0, 0], sib)

    def relay_y(r):
        return remote(feats.at[2, half(r, 0)], feats.at[6, half(r, 0)],
                      ssem.at[6, r, 0], rsem.at[6, r, 0], yn)

    def relay_x(r):
        return remote(feats.at[4, half(r, 1)], feats.at[6, half(r, 1)],
                      ssem.at[6, r, 1], rsem.at[6, r, 1], xn)

    def direct(s):
        return remote(h, feats.at[s], ssem.at[s, 0, 0], rsem.at[s, 0, 0], lax.rem(me + s, n))

    if grid:
        own_sib().start()
        for r in range(CHUNKS):
            to_x(r).start()
            to_y(r).start()
    else:
        def dstart(s, c):
            direct(s).start()
            return c
        lax.fori_loop(1, n, dstart, 0)

    lane = lax.broadcasted_iota(jnp.int32, (1, LANES), 1)
    sums = jnp.zeros((1, LANES), jnp.float32)
    squares = jnp.zeros((1, LANES), jnp.float32)
    total_len = 0
    for i in range(nr):
        score = rew[i].astype(jnp.float32)
        hit = lane == gid[i]
        sums = sums + jnp.where(hit, score, 0.0)
        squares = squares + jnp.where(hit, score * score, 0.0)
        total_len = total_len + jnp.clip(lens[i], 0, seq)
    count = jnp.zeros((1, LANES), jnp.float32) + total_len.astype(jnp.float32)
    dpa[my] = jnp.concatenate(
        [sums, squares, count, jnp.zeros((5, LANES), jnp.float32)], axis=0)

    lane_sq = lax.broadcasted_iota(jnp.int32, (LANES, LANES), 1)
    for q in range(nq):
        ids = jnp.broadcast_to(tg[q:q + 1, :] - me * width, (LANES, LANES))
        tcol[q * LANES:(q + 1) * LANES, :] = jnp.transpose(ids) - lane_sq

    for s in range(1, dpn):
        todp(dpa, dpa_s, dpa_r, lax.rem(my + s, dpn)).start()

    def mm(at, size, slots, first):
        for n0 in range(0, width, TILE):
            n1 = min(width, n0 + TILE)
            v = None if first else acc[pl.ds(at, size), n0:n1]
            for s in slots:
                d = jnp.dot(feats[s, pl.ds(at, size), :], wv[s, :, n0:n1],
                            preferred_element_type=jnp.float32)
                v = d if v is None else v + d
            acc[pl.ds(at, size), n0:n1] = v

    step = 16

    def stats_block(b, c):
        at = pl.multiple_of(b * step, step)
        cols = [acc[pl.ds(at, step), j:j + LANES] for j in range(0, width, LANES)]
        top = functools.reduce(jnp.maximum, cols)
        want = tcol[pl.ds(at, step), :]
        total = moment = pick = jnp.zeros((step, LANES), jnp.float32)
        for j, v in enumerate(cols):
            e = jnp.exp(v - top)
            total = total + e
            moment = moment + e * v
            pick = jnp.where(want == j * LANES, v, pick)
        part[0, pl.ds(at, step), :] = top
        part[1, pl.ds(at, step), :] = total
        part[2, pl.ds(at, step), :] = moment
        part[3, pl.ds(at, step), :] = pick
        return c

    def stats_rows(q):
        at = pl.multiple_of(q * LANES, LANES)
        lax.fori_loop(q * (LANES // step), (q + 1) * (LANES // step), stats_block, 0)
        m, t, mo, pk = (jnp.transpose(part[i, pl.ds(at, LANES), :]) for i in range(4))
        top = jnp.max(m, axis=0, keepdims=True)
        scale = jnp.exp(m - top)
        st[me, q] = jnp.concatenate(
            [top, jnp.sum(t * scale, axis=0, keepdims=True),
             jnp.sum(mo * scale, axis=0, keepdims=True), jnp.sum(pk, axis=0, keepdims=True),
             jnp.zeros((4, LANES), jnp.float32)], axis=0)

    hcopy.wait()
    if grid:
        wcopy(0, owners[0]).wait()
        own_sib().wait_recv()
        wcopy(1, owners[1]).wait()

        def own(r, c):
            mm(pl.multiple_of(r * rows, rows), rows, (0, 1), True)
            return c
        lax.fori_loop(0, CHUNKS, own, 0)
        for s in (2, 4, 3, 5):
            wcopy(s, owners[s]).wait()

        def sides(r, c):
            at = pl.multiple_of(r * rows, rows)
            to_x(r).wait_recv()
            to_y(r).wait_recv()
            relay_y(r).start()
            relay_x(r).start()
            to_sib(2, r).start()
            to_sib(4, r).start()
            mm(at, rows, (2, 4), False)
            to_sib(2, r).wait_recv()
            to_sib(4, r).wait_recv()
            mm(at, rows, (3, 5), False)
            return c
        lax.fori_loop(0, CHUNKS, sides, 0)
        for s in (6, 7):
            wcopy(s, owners[s]).wait()

        def corner(r, c):
            at = pl.multiple_of(r * rows, rows)
            relay_y(r).wait_recv()
            relay_x(r).wait_recv()
            to_sib(6, r).start()
            mm(at, rows, (6,), False)
            to_sib(6, r).wait_recv()
            mm(at, rows, (7,), False)
            for q in range(rows // LANES):
                stats_rows(r * (rows // LANES) + q)
            return c
        lax.fori_loop(0, CHUNKS, corner, 0)
    else:
        wcopy(0, me).wait()

        def first(r, c):
            mm(pl.multiple_of(r * rows, rows), rows, (0,), True)
            return c
        lax.fori_loop(0, CHUNKS, first, 0)

        def others(s, c):
            wcopy(s, lax.rem(me - s + n, n)).wait()
            direct(s).wait_recv()

            def inner(r, c2):
                mm(pl.multiple_of(r * rows, rows), rows, (s,), False)
                return c2
            lax.fori_loop(0, CHUNKS, inner, 0)
            return c
        lax.fori_loop(1, n, others, 0)

        def every(q, c):
            stats_rows(q)
            return c
        lax.fori_loop(0, nq, every, 0)

    def share(s):
        dev = lax.rem(me + s, n)
        return remote(st.at[me], st.at[me], st_s.at[s], st_r.at[me], dev)

    def shared(s):
        src = lax.rem(me + s, n)
        return remote(st.at[src], st.at[src], st_s.at[s], st_r.at[src], src)

    for s in range(1, n):
        share(s).start()

    for s in range(1, dpn):
        src = lax.rem(my + s, dpn)
        pltpu.make_async_remote_copy(
            src_ref=dpa.at[src], dst_ref=dpa.at[src], send_sem=dpa_s.at[src],
            recv_sem=dpa_r.at[src], device_id=(src, me), device_id_type=MESH).wait_recv()
    gathered = jnp.sum(dpa[...], axis=0)
    mean = gathered[0:1, :] / GROUP
    spread = jnp.sqrt(jnp.maximum(gathered[1:2, :] / GROUP - mean * mean, 0.0))
    count_all = gathered[2:3, :]
    roll = lax.broadcasted_iota(jnp.int32, (nr, LANES), 0)
    lanes = lax.broadcasted_iota(jnp.int32, (nr, LANES), 1)
    group = jnp.zeros((nr, LANES), jnp.int32)
    length = jnp.zeros((nr, LANES), jnp.int32)
    score = jnp.zeros((nr, LANES), jnp.float32)
    for i in range(nr):
        group = jnp.where(roll == i, gid[i], group)
        length = jnp.where(roll == i, lens[i], length)
        score = jnp.where(roll == i, rew[i].astype(jnp.float32), score)
    member = lanes == group
    mean_r = jnp.sum(jnp.where(member, mean, 0.0), axis=1, keepdims=True)
    spread_r = jnp.sum(jnp.where(member, spread, 0.0), axis=1, keepdims=True)
    adv_r = (score - mean_r) / jnp.maximum(spread_r, 1.0)
    advs, masks = [], []
    for q in range(nq):
        place = lanes + q * LANES - roll * seq
        inside = (place >= 0) & (place < seq)
        a = jnp.sum(jnp.where(inside, adv_r, 0.0), axis=0, keepdims=True)
        mk = jnp.sum(jnp.where(inside & (place < length), 1.0, 0.0), axis=0, keepdims=True)
        advs.append(a)
        masks.append(mk)
        adv[q:q + 1, :] = a

    for s in range(1, n):
        shared(s).wait_recv()
    numer = jnp.zeros((1, LANES), jnp.float32)
    for q in range(nq):
        a = st[:, q]
        top = jnp.max(a[:, 0:1, :], axis=0)
        scale = jnp.exp(a[:, 0:1, :] - top[None])
        total = jnp.sum(a[:, 1:2, :] * scale, axis=0)
        moment = jnp.sum(a[:, 2:3, :] * scale, axis=0)
        pick = jnp.sum(a[:, 3:4, :], axis=0)
        lse = top + jnp.log(total)
        lp = pick - lse
        en = lse - moment / total
        tok[q:q + 1, :] = lp
        ent[q:q + 1, :] = en
        ratio = jnp.exp(jnp.clip(lp - olp[q:q + 1, :], -20.0, 20.0))
        sur = -jnp.minimum(ratio * advs[q], jnp.clip(ratio, 0.8, 1.2) * advs[q])
        shift = jnp.clip(rlp[q:q + 1, :] - lp, -20.0, 20.0)
        div = jnp.exp(shift) - shift - 1.0
        numer = numer + masks[q] * (sur + 0.04 * div - 0.01 * en)
    dpb[my] = jnp.broadcast_to(numer, (8, LANES))
    for s in range(1, dpn):
        todp(dpb, dpb_s, dpb_r, lax.rem(my + s, dpn)).start()

    if grid:
        own_sib().wait_send()

        def drain(r, c):
            to_x(r).wait_send()
            to_y(r).wait_send()
            relay_y(r).wait_send()
            relay_x(r).wait_send()
            for s in (2, 4, 6):
                to_sib(s, r).wait_send()
            return c
        lax.fori_loop(0, CHUNKS, drain, 0)
    else:
        def ddrain(s, c):
            direct(s).wait_send()
            return c
        lax.fori_loop(1, n, ddrain, 0)
    for s in range(1, n):
        share(s).wait_send()
    for s in range(1, dpn):
        todp(dpa, dpa_s, dpa_r, lax.rem(my + s, dpn)).wait_send()
    for s in range(1, dpn):
        src = lax.rem(my + s, dpn)
        pltpu.make_async_remote_copy(
            src_ref=dpb.at[src], dst_ref=dpb.at[src], send_sem=dpb_s.at[src],
            recv_sem=dpb_r.at[src], device_id=(src, me), device_id_type=MESH).wait_recv()
    ratio = jnp.sum(dpb[:, 0:1, :], axis=0)
    loss[0] = jnp.sum(ratio) / jnp.max(count_all)
    for s in range(1, dpn):
        todp(dpb, dpb_s, dpb_r, lax.rem(my + s, dpn)).wait_send()


def per_device(n, dpn, hidden, weight, targets, old_logprob, ref_logprob, lengths, rewards, group_ids):
    tokens, kdim = hidden.shape
    width = weight.shape[1]
    nq = tokens // LANES
    anyspec = pl.BlockSpec(memory_space=pl.ANY)
    vmem = pl.BlockSpec(memory_space=pltpu.VMEM)
    smem = pl.BlockSpec(memory_space=pltpu.SMEM)
    dma = pltpu.SemaphoreType.DMA
    tile = jax.ShapeDtypeStruct((nq, LANES), jnp.float32)
    tok, ent, adv, loss = pl.pallas_call(
        functools.partial(kernel, n, dpn),
        out_shape=(tile, tile, tile, jax.ShapeDtypeStruct((1,), jnp.float32)),
        in_specs=[anyspec, anyspec, vmem, vmem, vmem, smem, smem, smem],
        out_specs=(vmem, vmem, vmem, smem),
        scratch_shapes=[
            pltpu.VMEM((n, tokens, kdim), jnp.bfloat16),
            pltpu.VMEM((n, kdim, width), jnp.bfloat16),
            pltpu.VMEM((tokens, width), jnp.float32),
            pltpu.VMEM((tokens, LANES), jnp.int32),
            pltpu.VMEM((4, tokens, LANES), jnp.float32),
            pltpu.VMEM((n, nq, 8, LANES), jnp.float32),
            pltpu.VMEM((dpn, 8, LANES), jnp.float32),
            pltpu.VMEM((dpn, 8, LANES), jnp.float32),
            dma, dma((n,)), dma((n, CHUNKS, 2)), dma((n, CHUNKS, 2)),
            dma((n,)), dma((n,)), dma((dpn,)), dma((dpn,)), dma((dpn,)), dma((dpn,)),
        ],
        compiler_params=pltpu.CompilerParams(
            collective_id=0, has_side_effects=True, vmem_limit_bytes=60 * 1024 * 1024),
        name="policy_loss",
    )(hidden, weight, targets.reshape(nq, LANES), old_logprob.reshape(nq, LANES),
      ref_logprob.reshape(nq, LANES), lengths, rewards, group_ids)
    return tok.reshape(tokens), ent.reshape(tokens), adv.reshape(tokens), loss.reshape(())


def solution(mesh):
    return jax.shard_map(
        functools.partial(per_device, mesh.shape["vocab"], mesh.shape["dp"]),
        mesh=mesh,
        in_specs=(
            P("dp", "vocab"),
            P(None, "vocab"),
            P("dp"),
            P("dp"),
            P("dp"),
            P("dp"),
            P("dp"),
            P("dp"),
        ),
        out_specs=(P("dp"), P("dp"), P("dp"), P()),
        check_vma=False,
    )
```

time: 128 us -> 52.6 us (0.41)
  blocking collectives: 51.1 us -> 0 us
  Pallas kernels: 0 us -> 46.2 us
  waiting for transfers between devices: 27.1 us -> 0 us
  matrix products: 25.3 us -> 0 us
  between operations: 16.5 us -> 2.38 us
  other arithmetic: 7.03 us -> 0 us
  local copies, waits for them, and re-layouts: 0.25 us -> 3.72 us
    pallas_call x0 -> x1, Pallas kernels: none -> 46.2 us  [per_device(): pl.pallas_call(functools.partial(kernel, n, dpn), out_shape=(tile, tile,...]
    psum x3 -> x0, blocking collectives: 37.8 us -> none  [the longest x1 13.5 us: per_device(): sums, squares = lax.psum((part_sums, part_squares), 'dp')]
    all_gather x1 -> x0, waiting for transfers between devices: 26.4 us -> none  [per_device(): features_all = lax.all_gather(hidden, 'vocab', axis=1, tiled=True)]
    dot_general x5 -> x0, matrix products: 25.3 us -> none  [the longest x1 21.8 us: per_device(): logits = jnp.dot(features_all, weight, preferred_element_type=jnp.float32)]
    pmax x1 -> x0, blocking collectives: 13.2 us -> none  [per_device(): top = lax.pmax(local_top, 'vocab')]
    reduce_sum x3 -> x0, other arithmetic: 6.29 us -> none  [the longest x1 3.7 us: per_device(): jnp.sum(scaled * logits, axis=1)]
    unnamed x8 -> x3, local copies, waits for them, and re-layouts: 0.01 us -> 3.72 us
  transfers between devices with their start and end apart: 1 -> 0, of which waited for: 1 -> 0; matrix products, arithmetic and copies ran while one was open for 5% -> 0% of each run, Pallas kernels for 0% -> 0%
where the time goes in v1:
time: 52.6 us; the launch traced here: 52.3 us
  Pallas kernels  46.2 us (88%)
  local copies, waits for them, and re-layouts  3.72 us (7%)
  between operations  2.38 us (5%)
    pallas_call x1, Pallas kernels, per_device(): pl.pallas_call(functools.partial(kernel, n, dpn), out_shape=(tile, tile,...  46.2 us
    unnamed x3, local copies, waits for them, and re-layouts  3.72 us

profile of v1, /device:TPU:0, one launch (start us, length us, event | category | flops | bytes accessed | tf_op | source)
XLA Modules:
  0.0 52.3 jit_solution(5011320645007218696)
XLA Ops:
  0.6 46.2 %policy_loss.1 = (f32[4,128]{1,0:T(4,128)}, f32[4,128]{1,0:T(4,128)}, f32[4,128]{1,0:T(4,128)}, f32[1]{0:T(128)}) custom-call(bf16[512,640]{1,0:T(8,128)(2,1)} %h.1, bf16[5120,2432]{1,0:T(8,128)(2,1)} %w.1, s32[4,128]{1,0:T(4,128)} %bitcast.7, f32[4,128]{1,0:T(4,128)} %bitcast.8, f32[4,128]{1,0:T(4,128)} %bitcast.9, s32[8]{0:T(128)} %lens.1, s32[8]{0:T(128)} %rew.1, ...), custom_call_target="tpu_custom_call" | custom-call | tf_op jit(solution)/shard_map/policy_loss/pallas_call | solution.py:348
  46.8 1.2 %copy.16 = f32[512]{0:T(512)} copy(f32[512]{0:T(512)} %bitcast.12) | data formatting | bytes 4096
  48.1 1.2 %copy.17 = f32[512]{0:T(512)} copy(f32[512]{0:T(512)} %bitcast.11) | data formatting | bytes 4096
  49.3 1.2 %copy.18 = f32[512]{0:T(512)} copy(f32[512]{0:T(512)} %bitcast.10) | data formatting | bytes 4096

commit v2 on v1

--- a/solution.py
+++ b/solution.py
@@ -9,12 +9,12 @@
 
 GROUP = 8
 LANES = 128
-CHUNKS = 4
+CHUNKS = 2
 TILE = 512
 MESH = pl.DeviceIdType.MESH
 
 
-def kernel(n, dpn, h, w, tg, olp, rlp, lens, rew, gid, tok, ent, adv, loss,
+def kernel(n, dpn, h, w, tg, olp, rlp, lens, rew, gid, res, loss,
            feats, wv, acc, tcol, part, st, dpa, dpb,
            hsem, wsem, ssem, rsem, st_s, st_r, dpa_s, dpa_r, dpb_s, dpb_r):
     me = lax.axis_index("vocab")
@@ -23,6 +23,7 @@
     width = w.shape[1]
     nq = tokens // LANES
     nr = lens.shape[0]
+    tok, ent, adv = res.at[0], res.at[1], res.at[2]
     seq = tokens // nr
     grid = n == 8
     rows = tokens // CHUNKS
@@ -53,7 +54,7 @@
     hcopy = pltpu.make_async_copy(h, feats.at[0], hsem)
     hcopy.start()
     if grid:
-        for s in range(n):
+        for s in range(2):
             wcopy(s, owners[s]).start()
     else:
         def wstart(s, c):
@@ -174,14 +175,27 @@
     hcopy.wait()
     if grid:
         wcopy(0, owners[0]).wait()
+        wcopy(2, owners[2]).start()
+
+        def own(r, c):
+            mm(pl.multiple_of(r * rows, rows), rows, (0,), True)
+            return c
+        lax.fori_loop(0, CHUNKS, own, 0)
         own_sib().wait_recv()
         wcopy(1, owners[1]).wait()
-
-        def own(r, c):
-            mm(pl.multiple_of(r * rows, rows), rows, (0, 1), True)
-            return c
-        lax.fori_loop(0, CHUNKS, own, 0)
-        for s in (2, 4, 3, 5):
+        wcopy(4, owners[4]).start()
+        wcopy(3, owners[3]).start()
+
+        def pair(r, c):
+            mm(pl.multiple_of(r * rows, rows), rows, (1,), False)
+            return c
+        lax.fori_loop(0, CHUNKS, pair, 0)
+        wcopy(2, owners[2]).wait()
+        wcopy(5, owners[5]).start()
+        wcopy(6, owners[6]).start()
+        wcopy(4, owners[4]).wait()
+        wcopy(7, owners[7]).start()
+        for s in (3, 5):
             wcopy(s, owners[s]).wait()
 
         def sides(r, c):
@@ -344,12 +358,12 @@
     vmem = pl.BlockSpec(memory_space=pltpu.VMEM)
     smem = pl.BlockSpec(memory_space=pltpu.SMEM)
     dma = pltpu.SemaphoreType.DMA
-    tile = jax.ShapeDtypeStruct((nq, LANES), jnp.float32)
-    tok, ent, adv, loss = pl.pallas_call(
+    res, loss = pl.pallas_call(
         functools.partial(kernel, n, dpn),
-        out_shape=(tile, tile, tile, jax.ShapeDtypeStruct((1,), jnp.float32)),
+        out_shape=(jax.ShapeDtypeStruct((3, nq, LANES), jnp.float32),
+                   jax.ShapeDtypeStruct((1,), jnp.float32)),
         in_specs=[anyspec, anyspec, vmem, vmem, vmem, smem, smem, smem],
-        out_specs=(vmem, vmem, vmem, smem),
+        out_specs=(vmem, smem),
         scratch_shapes=[
             pltpu.VMEM((n, tokens, kdim), jnp.bfloat16),
             pltpu.VMEM((n, kdim, width), jnp.bfloat16),
@@ -367,7 +381,7 @@
         name="policy_loss",
     )(hidden, weight, targets.reshape(nq, LANES), old_logprob.reshape(nq, LANES),
       ref_logprob.reshape(nq, LANES), lengths, rewards, group_ids)
-    return tok.reshape(tokens), ent.reshape(tokens), adv.reshape(tokens), loss.reshape(())
+    return res[0].reshape(tokens), res[1].reshape(tokens), res[2].reshape(tokens), loss.reshape(())
 
 
 def solution(mesh):

time: 52.6 us -> 47.8 us (0.909)
  local copies, waits for them, and re-layouts: 3.72 us -> 1.26 us
  Pallas kernels: 46.2 us -> 43.9 us
    unnamed x3 -> x0, local copies, waits for them, and re-layouts: 3.72 us -> none
    pallas_call x1, Pallas kernels: 46.2 us -> 43.9 us  [per_device(): pl.pallas_call(functools.partial(kernel, n, dpn), out_shape=(jax.ShapeDty...]
    another operation x0 -> x1, local copies, waits for them, and re-layouts: none -> 1.26 us  [per_device(): res[2].reshape(tokens)]
where the time goes in v2:
time: 47.8 us; the launch traced here: 47.6 us
  Pallas kernels  43.9 us (92%)
  between operations  2.4 us (5%)
  local copies, waits for them, and re-layouts  1.26 us (3%)
    pallas_call x1, Pallas kernels, per_device(): pl.pallas_call(functools.partial(kernel, n, dpn), out_shape=(jax.ShapeDty...  43.9 us
    another operation x1, local copies, waits for them, and re-layouts, per_device(): res[2].reshape(tokens)  1.26 us

profile of v2, /device:TPU:0, one launch (start us, length us, event | category | flops | bytes accessed | tf_op | source)
XLA Modules:
  0.0 47.6 jit_solution(17966812689325148158)
XLA Ops:
  0.6 43.9 %policy_loss.1 = (f32[3,4,128]{2,1,0:T(4,128)}, f32[1]{0:T(128)}) custom-call(bf16[512,640]{1,0:T(8,128)(2,1)} %h.1, bf16[5120,2432]{1,0:T(8,128)(2,1)} %w.1, s32[4,128]{1,0:T(4,128)} %bitcast.10, f32[4,128]{1,0:T(4,128)} %bitcast.11, f32[4,128]{1,0:T(4,128)} %bitcast.12, s32[8]{0:T(128)} %lens.1, s32[8]{0:T(128)} %rew.1, s32[8]{0:T(128)} %gid.1), custom_call_target="tpu_custom_call" | custom-call | tf_op jit(solution)/shard_map/policy_loss/pallas_call | solution.py:361
  44.5 1.3 %slice_bitcast_fusion = (f32[512]{0:T(512)}, f32[512]{0:T(512)}, f32[512]{0:T(512)}) fusion(f32[3,4,128]{2,1,0:T(4,128)} %get-tuple-element.6), kind=kLoop, calls=%fused_computation | loop fusion | bytes 12288 | tf_op jit(solution)/shard_map/reshape;squeeze | solution.py:384
